TPU v7x, 32 devices: a whole 2x2x4 slice. The times are simulated.
32 devices in a mesh: ctx: 4 (over z), fsdp: 2 (over core), kvh: 4 (over y, x).
Axes of the slice: x: 2, y: 2, z: 4, core: 2. Of those that a mesh axis runs over, the one named last changes fastest.
Arguments:
- hidden: bfloat16 [2048, 4096], P(('ctx', 'fsdp'), 'kvh'), may hold values from -6 to 6
- key_value_matrix: bfloat16 [4096, 2048], P('fsdp', 'kvh'), may hold values from -0.09375 to 0.09375
- queries: bfloat16 [2048, 4096], P(('ctx', 'fsdp'), 'kvh')
- vertical_blocks: int32 [8, 8], P('kvh'), may hold values from 0 to 15, as said below
- slash_offsets: int32 [8, 2], P('kvh'), may hold values from 1 to 15, as said below
Outputs:
- attended: bfloat16 [2048, 4096], P(('ctx', 'fsdp'), 'kvh')
Inputs may be any that keep to these rules, and one draw needn't show every extreme that they name: `vertical_blocks`: the 8 entries of one head are distinct key blocks. `slash_offsets`: the 2 entries of one head are distinct block distances.
All inputs are finite; a program needn't handle non-finite values.
Results may differ from a plain program's by a relative error of at most 0.012.
The roundings to bfloat16 on the way count: a program that leaves them out, or rounds other values in their place, can miss the bound.
Values may be sent and summed in bfloat16 or wider, within the bound.
No kernel may reach another device: no remote copies, remote signals or barrier semaphores. Data moves between devices by JAX's collectives and lax.ppermute only.
A program may use at most 64 MiB of HBM per device.

v0:
```python
import jax
import jax.numpy as jnp
from jax import lax
from jax.sharding import PartitionSpec as P

HEAD_DIMENSION = 128
BLOCK_TOKENS = 128


def broadcast(value, axis, source):
    kept = jnp.where(lax.axis_index(axis) == source, value, 0).astype(value.dtype)
    return lax.psum(kept, axis)


def from_behind(value, axis, by):
    size = lax.axis_size(axis)
    pairs = [(i, i + by) for i in range(size) if 0 <= i + by < size]
    return lax.ppermute(value, axis, pairs)


def rotate_keys(raw_keys, positions):
    half = raw_keys.shape[-1] // 2
    frequency = jnp.power(
        500000.0, -(jnp.arange(half, dtype=jnp.float32) * 2.0 / raw_keys.shape[-1])
    )
    angle = positions[:, None] * frequency[None, :]
    cosine = jnp.cos(angle)[:, None, :]
    sine = jnp.sin(angle)[:, None, :]
    first_half = raw_keys[..., :half]
    second_half = raw_keys[..., half:]
    return jnp.concatenate(
        [first_half * cosine - second_half * sine, second_half * cosine + first_half * sine],
        axis=-1,
    )


def per_device(hidden, key_value_matrix, queries, vertical_blocks, slash_offsets):
    tok_rows = hidden.shape[0]
    head_size = HEAD_DIMENSION
    block_rows = BLOCK_TOKENS
    local_count = tok_rows // block_rows
    local_heads = key_value_matrix.shape[1] // (2 * head_size)
    gathered = lax.all_gather(hidden, "kvh", axis=1, tiled=True)
    projected_tokens = jnp.dot(
        gathered,
        lax.all_gather(key_value_matrix, "fsdp", axis=0, tiled=True),
        preferred_element_type=jnp.float32,
    )
    projected_tokens = projected_tokens.reshape(tok_rows, local_heads, 2, head_size)
    position = lax.axis_index(("ctx", "fsdp"))
    positions = (position * tok_rows + jnp.arange(tok_rows, dtype=jnp.int32)).astype(jnp.float32)
    key_tensor = rotate_keys(projected_tokens[:, :, 0], positions).astype(jnp.bfloat16)
    value_tensor = projected_tokens[:, :, 1].astype(jnp.bfloat16)
    own_blocks = (
        jnp.stack([key_tensor, value_tensor], axis=2)
        .reshape(local_count, block_rows, local_heads, 2, head_size)
        .transpose(2, 0, 1, 3, 4)
    )
    shards = lax.axis_size(("ctx", "fsdp"))
    vertical_count = vertical_blocks.shape[1]
    slash_count = slash_offsets.shape[1]

    def fetch_block(counter, buffer):
        head_index = counter // vertical_count
        slot_index = counter % vertical_count
        wanted = vertical_blocks[head_index, slot_index]
        head_blocks = lax.dynamic_index_in_dim(own_blocks, head_index, 0, keepdims=False)
        outgoing = lax.dynamic_index_in_dim(head_blocks, wanted % local_count, 0, keepdims=False)
        received = broadcast(outgoing, ("ctx", "fsdp"), wanted // local_count)
        return buffer.at[head_index, slot_index].set(received)

    start_buffer = jnp.zeros((local_heads, vertical_count) + own_blocks.shape[2:], jnp.bfloat16)
    vertical_kv = lax.fori_loop(0, local_heads * vertical_count, fetch_block, start_buffer)
    device_shift = slash_offsets // local_count
    remainder = slash_offsets % local_count
    moving = jnp.broadcast_to(
        own_blocks[:, None], (local_heads, slash_count) + own_blocks.shape[1:]
    )
    for digit in range((shards - 1).bit_length()):
        shifted = from_behind(moving, ("ctx", "fsdp"), 1 << digit)
        chosen = device_shift // (1 << digit) % 2 == 1
        moving = jnp.where(chosen[:, :, None, None, None, None], shifted, moving)
    earlier = from_behind(moving, ("ctx", "fsdp"), 1)
    extended = jnp.concatenate([earlier, moving], axis=2)
    local_ids = jnp.arange(local_count, dtype=jnp.int32)
    wanted_index = local_count + local_ids[None, None, :] - remainder[:, :, None]
    selector = (wanted_index[..., None] == jnp.arange(2 * local_count, dtype=jnp.int32)).astype(
        jnp.bfloat16
    )
    slash_kv = jnp.einsum(
        "hnbk,hnkucd->hnbucd", selector, extended, preferred_element_type=jnp.float32
    ).astype(jnp.bfloat16)
    slot_ids = jnp.arange(1 + vertical_count + slash_count, dtype=jnp.int32)
    token_ids = jnp.arange(block_rows, dtype=jnp.int32)
    token_ok = (slot_ids[None, :, None] > 0) | (
        token_ids[None, None, :] <= token_ids[:, None, None]
    )
    group_size = queries.shape[1] // (local_heads * head_size)
    query_blocks = queries.reshape(local_count, block_rows, local_heads, group_size, head_size)
    scale = head_size ** (-0.5)

    def attend(item):
        own_one, slash_one, query_one, local_index = item
        mask_block = position * local_count + local_index
        all_blocks = jnp.concatenate([own_one[:, None], vertical_kv, slash_one], axis=1)
        key_sel = all_blocks[:, :, :, 0]
        value_sel = all_blocks[:, :, :, 1]
        vertical_allowed = (vertical_blocks < mask_block) & jnp.logical_not(
            jnp.any(
                (mask_block - vertical_blocks)[:, :, None] == slash_offsets[:, None, :], axis=-1
            )
        )
        slash_allowed = slash_offsets <= mask_block
        valid_mask = jnp.concatenate(
            [jnp.ones((local_heads, 1), dtype=bool), vertical_allowed, slash_allowed], axis=1
        )
        allowed = valid_mask[:, None, None, :, None] & token_ok[None, None]
        scores = (
            jnp.einsum("thgd,hsud->hgtsu", query_one, key_sel, preferred_element_type=jnp.float32)
            * scale
        )
        scores = jnp.where(allowed, scores, -jnp.inf)
        largest = jnp.max(scores, axis=(3, 4), keepdims=True)
        expo = jnp.exp(scores - largest)
        probs = (expo / jnp.sum(expo, axis=(3, 4), keepdims=True)).astype(jnp.bfloat16)
        result = jnp.einsum(
            "hgtsu,hsud->thgd", probs, value_sel, preferred_element_type=jnp.float32
        )
        return result.astype(jnp.bfloat16).reshape(block_rows, local_heads * group_size * head_size)

    inputs = (
        own_blocks.transpose(1, 0, 2, 3, 4),
        slash_kv.transpose(2, 0, 1, 3, 4, 5),
        query_blocks,
        local_ids,
    )
    outputs = lax.map(attend, inputs)
    return outputs.reshape(tok_rows, local_heads * group_size * head_size)


def solution(mesh):
    return jax.shard_map(
        per_device,
        mesh=mesh,
        in_specs=(
            P(("ctx", "fsdp"), "kvh"),
            P("fsdp", "kvh"),
            P(("ctx", "fsdp"), "kvh"),
            P("kvh", None),
            P("kvh", None),
        ),
        out_specs=P(("ctx", "fsdp"), "kvh"),
        check_vma=False,
    )
```

profile of v0, /device:TPU:0, one launch (start us, length us, event | category | flops | bytes accessed | tf_op | source)
XLA Modules:
  0.0 1108.5 jit_solution(16996056453087566824)
XLA Ops:
  6.5 0.7 all-gather.3.cloned.1.call-update
  7.3 0.7 all-gather.5.cloned.1.call-update
  8.4 38.8 %all-gather.3.cloned.1.call-done = bf16[256,4096]{1,0:T(8,128)(2,1)} async-done(((bf16[256,1024]{1,0:T(8,128)(2,1)}), bf16[256,4096]{1,0:T(8,128)(2,1)}) %all-gather.3.cloned.1.call-update) | async-done | bytes 2097168 | tf_op jit(solution)/shard_map/all_gather | solution.py:43
  47.1 15.2 %all-gather.5.cloned.1.call-done = bf16[4096,512]{1,0:T(8,128)(2,1)} async-done(((bf16[2048,512]{1,0:T(8,128)(2,1)}), bf16[4096,512]{1,0:T(8,128)(2,1)}) %all-gather.5.cloned.1.call-update) | async-done | bytes 4194320 | tf_op jit(solution)/shard_map/all_gather | solution.py:46
  62.4 4.1 fusion.22
  68.7 2.2 collective-permute-start
  70.9 1.4 collective-permute-done
  73.0 10.5 collective-permute-start.1
  83.6 10.4 collective-permute-done.1
  94.0 0.8 broadcast_select_fusion.3
  94.8 5.3 collective-permute-start.2
  100.6 9.2 collective-permute-done.2
  110.4 2.1 collective-permute-start.3
  113.5 2.4 fusion.10
  116.3 971.2 %while.30 = (s32[]{:T(128)}, bf16[2,8,128,2,128]{4,2,1,0,3:T(8,128)(2,1)S(1)}, s32[2,8]{1,0:T(2,128)S(1)}, bf16[2,2,128,2,128]{4,3,2,1,0:T(2,128)(2,1)S(1)}, s32...) while((s32[]{:T(128)}, ...), condition=%wide.region_3.4_spmd, body=%wide.region_0.3_spmd.sunk | while | flops 98376 | bytes 983881 | solution.py:73
  119.6 0.7 broadcast_select_fusion.7
  121.0 72.3 %all-reduce.2.cloned.1.call-done = bf16[1,1,128,2,128]{4,3,2,1,0:T(2,128)(2,1)} async-done(((bf16[1,1,128,2,128]{4,3,2,1,0:T(2,128)(2,1)}), bf16[1,1,128,2,128]{4,3,2,1,0:T(2,128)(2,1)}) %all-reduce.2.cloned.1.call-update) | async-done | bytes 65552 | tf_op jit(solution)/shard_map/while/body/eval_jaxpr/psum | solution.py:12
  193.4 1.6 broadcast_select_fusion.8
  198.2 0.7 broadcast_select_fusion.7
  199.7 53.2 %all-reduce.2.cloned.1.call-done = bf16[1,1,128,2,128]{4,3,2,1,0:T(2,128)(2,1)} async-done(((bf16[1,1,128,2,128]{4,3,2,1,0:T(2,128)(2,1)}), bf16[1,1,128,2,128]{4,3,2,1,0:T(2,128)(2,1)}) %all-reduce.2.cloned.1.call-update) | async-done | bytes 65552 | tf_op jit(solution)/shard_map/while/body/eval_jaxpr/psum | solution.py:12
  252.9 1.6 broadcast_select_fusion.8
  257.7 0.7 broadcast_select_fusion.7
  259.2 53.2 %all-reduce.2.cloned.1.call-done = bf16[1,1,128,2,128]{4,3,2,1,0:T(2,128)(2,1)} async-done(((bf16[1,1,128,2,128]{4,3,2,1,0:T(2,128)(2,1)}), bf16[1,1,128,2,128]{4,3,2,1,0:T(2,128)(2,1)}) %all-reduce.2.cloned.1.call-update) | async-done | bytes 65552 | tf_op jit(solution)/shard_map/while/body/eval_jaxpr/psum | solution.py:12
  312.4 1.6 broadcast_select_fusion.8
  317.2 0.7 broadcast_select_fusion.7
  318.7 53.2 %all-reduce.2.cloned.1.call-done = bf16[1,1,128,2,128]{4,3,2,1,0:T(2,128)(2,1)} async-done(((bf16[1,1,128,2,128]{4,3,2,1,0:T(2,128)(2,1)}), bf16[1,1,128,2,128]{4,3,2,1,0:T(2,128)(2,1)}) %all-reduce.2.cloned.1.call-update) | async-done | bytes 65552 | tf_op jit(solution)/shard_map/while/body/eval_jaxpr/psum | solution.py:12
  371.9 1.6 broadcast_select_fusion.8
  376.7 0.7 broadcast_select_fusion.7
  378.2 53.2 %all-reduce.2.cloned.1.call-done = bf16[1,1,128,2,128]{4,3,2,1,0:T(2,128)(2,1)} async-done(((bf16[1,1,128,2,128]{4,3,2,1,0:T(2,128)(2,1)}), bf16[1,1,128,2,128]{4,3,2,1,0:T(2,128)(2,1)}) %all-reduce.2.cloned.1.call-update) | async-done | bytes 65552 | tf_op jit(solution)/shard_map/while/body/eval_jaxpr/psum | solution.py:12
  431.4 1.6 broadcast_select_fusion.8
  436.2 0.7 broadcast_select_fusion.7
  437.7 53.2 %all-reduce.2.cloned.1.call-done = bf16[1,1,128,2,128]{4,3,2,1,0:T(2,128)(2,1)} async-done(((bf16[1,1,128,2,128]{4,3,2,1,0:T(2,128)(2,1)}), bf16[1,1,128,2,128]{4,3,2,1,0:T(2,128)(2,1)}) %all-reduce.2.cloned.1.call-update) | async-done | bytes 65552 | tf_op jit(solution)/shard_map/while/body/eval_jaxpr/psum | solution.py:12
  490.9 1.6 broadcast_select_fusion.8
  495.7 0.7 broadcast_select_fusion.7
  497.2 53.2 %all-reduce.2.cloned.1.call-done = bf16[1,1,128,2,128]{4,3,2,1,0:T(2,128)(2,1)} async-done(((bf16[1,1,128,2,128]{4,3,2,1,0:T(2,128)(2,1)}), bf16[1,1,128,2,128]{4,3,2,1,0:T(2,128)(2,1)}) %all-reduce.2.cloned.1.call-update) | async-done | bytes 65552 | tf_op jit(solution)/shard_map/while/body/eval_jaxpr/psum | solution.py:12
  550.4 1.6 broadcast_select_fusion.8
  555.2 0.7 broadcast_select_fusion.7
  556.7 53.2 %all-reduce.2.cloned.1.call-done = bf16[1,1,128,2,128]{4,3,2,1,0:T(2,128)(2,1)} async-done(((bf16[1,1,128,2,128]{4,3,2,1,0:T(2,128)(2,1)}), bf16[1,1,128,2,128]{4,3,2,1,0:T(2,128)(2,1)}) %all-reduce.2.cloned.1.call-update) | async-done | bytes 65552 | tf_op jit(solution)/shard_map/while/body/eval_jaxpr/psum | solution.py:12
  609.9 1.6 broadcast_select_fusion.8
  616.2 53.2 %all-reduce.2.cloned.1.call-done = bf16[1,1,128,2,128]{4,3,2,1,0:T(2,128)(2,1)} async-done(((bf16[1,1,128,2,128]{4,3,2,1,0:T(2,128)(2,1)}), bf16[1,1,128,2,128]{4,3,2,1,0:T(2,128)(2,1)}) %all-reduce.2.cloned.1.call-update) | async-done | bytes 65552 | tf_op jit(solution)/shard_map/while/body/eval_jaxpr/psum | solution.py:12
  669.4 1.6 broadcast_select_fusion.8
  675.7 53.2 %all-reduce.2.cloned.1.call-done = bf16[1,1,128,2,128]{4,3,2,1,0:T(2,128)(2,1)} async-done(((bf16[1,1,128,2,128]{4,3,2,1,0:T(2,128)(2,1)}), bf16[1,1,128,2,128]{4,3,2,1,0:T(2,128)(2,1)}) %all-reduce.2.cloned.1.call-update) | async-done | bytes 65552 | tf_op jit(solution)/shard_map/while/body/eval_jaxpr/psum | solution.py:12
  728.9 1.6 broadcast_select_fusion.8
  735.2 53.2 %all-reduce.2.cloned.1.call-done = bf16[1,1,128,2,128]{4,3,2,1,0:T(2,128)(2,1)} async-done(((bf16[1,1,128,2,128]{4,3,2,1,0:T(2,128)(2,1)}), bf16[1,1,128,2,128]{4,3,2,1,0:T(2,128)(2,1)}) %all-reduce.2.cloned.1.call-update) | async-done | bytes 65552 | tf_op jit(solution)/shard_map/while/body/eval_jaxpr/psum | solution.py:12
  788.4 1.6 broadcast_select_fusion.8
  794.7 53.2 %all-reduce.2.cloned.1.call-done = bf16[1,1,128,2,128]{4,3,2,1,0:T(2,128)(2,1)} async-done(((bf16[1,1,128,2,128]{4,3,2,1,0:T(2,128)(2,1)}), bf16[1,1,128,2,128]{4,3,2,1,0:T(2,128)(2,1)}) %all-reduce.2.cloned.1.call-update) | async-done | bytes 65552 | tf_op jit(solution)/shard_map/while/body/eval_jaxpr/psum | solution.py:12
  847.9 1.6 broadcast_select_fusion.8
  854.2 53.2 %all-reduce.2.cloned.1.call-done = bf16[1,1,128,2,128]{4,3,2,1,0:T(2,128)(2,1)} async-done(((bf16[1,1,128,2,128]{4,3,2,1,0:T(2,128)(2,1)}), bf16[1,1,128,2,128]{4,3,2,1,0:T(2,128)(2,1)}) %all-reduce.2.cloned.1.call-update) | async-done | bytes 65552 | tf_op jit(solution)/shard_map/while/body/eval_jaxpr/psum | solution.py:12
  907.4 1.6 broadcast_select_fusion.8
  913.7 53.2 %all-reduce.2.cloned.1.call-done = bf16[1,1,128,2,128]{4,3,2,1,0:T(2,128)(2,1)} async-done(((bf16[1,1,128,2,128]{4,3,2,1,0:T(2,128)(2,1)}), bf16[1,1,128,2,128]{4,3,2,1,0:T(2,128)(2,1)}) %all-reduce.2.cloned.1.call-update) | async-done | bytes 65552 | tf_op jit(solution)/shard_map/while/body/eval_jaxpr/psum | solution.py:12
  966.9 1.6 broadcast_select_fusion.8
  973.2 53.2 %all-reduce.2.cloned.1.call-done = bf16[1,1,128,2,128]{4,3,2,1,0:T(2,128)(2,1)} async-done(((bf16[1,1,128,2,128]{4,3,2,1,0:T(2,128)(2,1)}), bf16[1,1,128,2,128]{4,3,2,1,0:T(2,128)(2,1)}) %all-reduce.2.cloned.1.call-update) | async-done | bytes 65552 | tf_op jit(solution)/shard_map/while/body/eval_jaxpr/psum | solution.py:12
  1026.4 1.6 broadcast_select_fusion.8
  1032.7 53.2 %all-reduce.2.cloned.1.call-done = bf16[1,1,128,2,128]{4,3,2,1,0:T(2,128)(2,1)} async-done(((bf16[1,1,128,2,128]{4,3,2,1,0:T(2,128)(2,1)}), bf16[1,1,128,2,128]{4,3,2,1,0:T(2,128)(2,1)}) %all-reduce.2.cloned.1.call-update) | async-done | bytes 65552 | tf_op jit(solution)/shard_map/while/body/eval_jaxpr/psum | solution.py:12
  1085.9 1.6 broadcast_select_fusion.8
  1087.5 14.2 %while.31 = (s32[]{:T(128)}, bf16[2,128,1024]{2,1,0:T(8,128)(2,1)}, bf16[2,2,128,2,128]{4,2,1,3,0:T(8,128)(2,1)S(1)}, bf16[2,2,2,128,2,128]{5,3,2,1,4,0:T(8,128)...) while((s32[]{:T(128)}, bf16[2,128,1024]{2,1,0:T(8,128)(2,1)}, ...), condition=%wide.region_8.9_spmd.clone, body=%wide.region_4.8_spmd.clone.sunk | while | flops 757610624 | bytes 30544560 | solution.py:137
  1089.8 0.9 fusion.30
  1090.7 1.3 fusion.31
  1092.0 1.6 fusion.32
  1093.8 0.8 copy-done.4
  1096.8 0.9 fusion.30
  1097.8 1.3 fusion.31
  1099.1 1.6 fusion.32
  1100.9 0.8 copy-done.4
  (199 shorter events, 38.4 us)
Async XLA Ops:
  6.5 40.6 %all-gather.3.cloned.1.call-start = ((), (), s32[]{:S(2)}) async-start(), calls=%async_computation | async-start | bytes 2621440 | tf_op jit(solution)/shard_map/all_gather | solution.py:43
  7.3 55.1 %all-gather.5.cloned.1.call-start = ((), (), s32[]{:S(2)}) async-start(), calls=%async_computation.1 | async-start | bytes 6291456 | tf_op jit(solution)/shard_map/all_gather | solution.py:46
  66.4 4.4 copy-start.2
  66.8 33.4 %copy-start = (bf16[256,1024]{1,0:T(8,128)(2,1)S(1)}, bf16[256,1024]{1,0:T(8,128)(2,1)}, u32[]{:S(2)}) copy-start(bf16[256,1024]{1,0:T(8,128)(2,1)} %param.13) | copy-start | bytes 1572868
  68.7 3.7 collective-permute-start
  73.0 21.0 %collective-permute-start.1 = (bf16[2,2,2,128,2,128]{5,2,4,3,1,0:T(2,128)(2,1)S(1)}, bf16[2,2,2,128,2,128]{5,2,4,3,1,0:T(2,128)(2,1)S(1)}, u32[]{:S(2)}, u32[]{:S(2)}) collective-permute-start(bf16[2,2,2,128,2,128]{5,2,4,3,1,0:T(2,128)(2,1)S(1)} %broadcast_select_fusion.2), channel_id=1, source_target_pairs={{0,8},{4,12},{8,16},{12,20},{16,24},{20,28},{1,9},{5,13},{9,17},{1... | collective-permute-start | bytes 1572872 | tf_op jit(solution)/shard_map/ppermute | solution.py:18
  94.8 15.0 %collective-permute-start.2 = (bf16[2,2,2,128,2,128]{5,2,4,3,1,0:T(2,128)(2,1)S(1)}, bf16[2,2,2,128,2,128]{5,2,4,3,1,0:T(2,128)(2,1)S(1)}, u32[]{:S(2)}, u32[]{:S(2)}) collective-permute-start(bf16[2,2,2,128,2,128]{5,2,4,3,1,0:T(2,128)(2,1)S(1)} %broadcast_select_fusion.3), channel_id=1, source_target_pairs={{0,16},{4,20},{8,24},{12,28},{1,17},{5,21},{9,25},{13,29},{2,18},{... | collective-permute-start | bytes 1572872 | tf_op jit(solution)/shard_map/ppermute | solution.py:18
  109.8 6.5 copy-start.1
  109.8 6.5 copy-start.5
  110.4 3.1 collective-permute-start.3
  116.3 77.1 %all-reduce.2.cloned.1.call-start = ((), (), s32[]{:S(2)}) async-start(), calls=%async_computation.2 | async-start | bytes 131072 | tf_op jit(solution)/shard_map/while/body/eval_jaxpr/psum | solution.py:12
  195.0 57.9 %all-reduce.2.cloned.1.call-start = ((), (), s32[]{:S(2)}) async-start(), calls=%async_computation.2 | async-start | bytes 131072 | tf_op jit(solution)/shard_map/while/body/eval_jaxpr/psum | solution.py:12
  254.5 57.9 %all-reduce.2.cloned.1.call-start = ((), (), s32[]{:S(2)}) async-start(), calls=%async_computation.2 | async-start | bytes 131072 | tf_op jit(solution)/shard_map/while/body/eval_jaxpr/psum | solution.py:12
  314.0 57.9 %all-reduce.2.cloned.1.call-start = ((), (), s32[]{:S(2)}) async-start(), calls=%async_computation.2 | async-start | bytes 131072 | tf_op jit(solution)/shard_map/while/body/eval_jaxpr/psum | solution.py:12
  373.5 57.9 %all-reduce.2.cloned.1.call-start = ((), (), s32[]{:S(2)}) async-start(), calls=%async_computation.2 | async-start | bytes 131072 | tf_op jit(solution)/shard_map/while/body/eval_jaxpr/psum | solution.py:12
  433.0 57.9 %all-reduce.2.cloned.1.call-start = ((), (), s32[]{:S(2)}) async-start(), calls=%async_computation.2 | async-start | bytes 131072 | tf_op jit(solution)/shard_map/while/body/eval_jaxpr/psum | solution.py:12
  492.5 57.9 %all-reduce.2.cloned.1.call-start = ((), (), s32[]{:S(2)}) async-start(), calls=%async_computation.2 | async-start | bytes 131072 | tf_op jit(solution)/shard_map/while/body/eval_jaxpr/psum | solution.py:12
  552.0 57.9 %all-reduce.2.cloned.1.call-start = ((), (), s32[]{:S(2)}) async-start(), calls=%async_computation.2 | async-start | bytes 131072 | tf_op jit(solution)/shard_map/while/body/eval_jaxpr/psum | solution.py:12
  611.5 57.9 %all-reduce.2.cloned.1.call-start = ((), (), s32[]{:S(2)}) async-start(), calls=%async_computation.2 | async-start | bytes 131072 | tf_op jit(solution)/shard_map/while/body/eval_jaxpr/psum | solution.py:12
  671.0 57.9 %all-reduce.2.cloned.1.call-start = ((), (), s32[]{:S(2)}) async-start(), calls=%async_computation.2 | async-start | bytes 131072 | tf_op jit(solution)/shard_map/while/body/eval_jaxpr/psum | solution.py:12
  730.5 57.9 %all-reduce.2.cloned.1.call-start = ((), (), s32[]{:S(2)}) async-start(), calls=%async_computation.2 | async-start | bytes 131072 | tf_op jit(solution)/shard_map/while/body/eval_jaxpr/psum | solution.py:12
  790.0 57.9 %all-reduce.2.cloned.1.call-start = ((), (), s32[]{:S(2)}) async-start(), calls=%async_computation.2 | async-start | bytes 131072 | tf_op jit(solution)/shard_map/while/body/eval_jaxpr/psum | solution.py:12
  849.5 57.9 %all-reduce.2.cloned.1.call-start = ((), (), s32[]{:S(2)}) async-start(), calls=%async_computation.2 | async-start | bytes 131072 | tf_op jit(solution)/shard_map/while/body/eval_jaxpr/psum | solution.py:12
  909.0 57.9 %all-reduce.2.cloned.1.call-start = ((), (), s32[]{:S(2)}) async-start(), calls=%async_computation.2 | async-start | bytes 131072 | tf_op jit(solution)/shard_map/while/body/eval_jaxpr/psum | solution.py:12
  968.5 57.9 %all-reduce.2.cloned.1.call-start = ((), (), s32[]{:S(2)}) async-start(), calls=%async_computation.2 | async-start | bytes 131072 | tf_op jit(solution)/shard_map/while/body/eval_jaxpr/psum | solution.py:12
  1028.0 57.9 %all-reduce.2.cloned.1.call-start = ((), (), s32[]{:S(2)}) async-start(), calls=%async_computation.2 | async-start | bytes 131072 | tf_op jit(solution)/shard_map/while/body/eval_jaxpr/psum | solution.py:12
  1092.0 1.8 copy-start.3
  1093.8 0.8 copy-start.4
  1099.1 1.8 copy-start.3
  1100.9 0.8 copy-start.4
Sparse Core Ops, SparseCore 0:
  9.2 37.8 all-gather.2
  48.7 13.6 all-gather.4
  120.4 72.9 all-reduce.1
  199.1 53.7 all-reduce.1
  258.6 53.7 all-reduce.1
  318.1 53.7 all-reduce.1
  377.6 53.7 all-reduce.1
  437.1 53.7 all-reduce.1
  496.6 53.7 all-reduce.1
  556.1 53.7 all-reduce.1
  615.6 53.7 all-reduce.1
  675.1 53.7 all-reduce.1
  734.6 53.7 all-reduce.1
  794.1 53.7 all-reduce.1
  853.6 53.7 all-reduce.1
  913.1 53.7 all-reduce.1
  972.6 53.7 all-reduce.1
  1032.1 53.7 all-reduce.1
where the time goes:
time: 1110 us
  waiting for transfers between devices  947 us (85%)
  other arithmetic  53.8 us (5%)
  loops' own time  43 us (4%)
  starting transfers between devices  20.8 us (2%)
  local copies, waits for them, and re-layouts  19 us (2%)
  between operations  13.7 us (1%)
  matrix products  11.5 us (1%)
    psum x16, waiting for transfers between devices, broadcast(): return lax.psum(kept, axis)  870 us
    another operation x1, loops' own time, per_device(): lax.fori_loop(0, local_heads * vertical_count, fetch_block, start_buffer)  41.5 us
    all_gather x1, waiting for transfers between devices, per_device(): gathered = lax.all_gather(hidden, 'kvh', axis=1, tiled=True)  38.8 us
    another operation x33, other arithmetic  35.5 us
  transfers between devices with their start and end apart: 22, of which 21 were waited for; matrix products, arithmetic and copies ran while one was open for 1% of the time, Pallas kernels for 0%

commit v1 on v0

--- a/solution.py
+++ b/solution.py
@@ -7,9 +7,14 @@
 BLOCK_TOKENS = 128
 
 
+def _store_unit(local_values, net_axis):
+    before = jnp.sum(lax.all_gather(local_values, net_axis), axis=0)
+    return before
+
+
 def broadcast(value, axis, source):
     kept = jnp.where(lax.axis_index(axis) == source, value, 0).astype(value.dtype)
-    return lax.psum(kept, axis)
+    return _store_unit(kept, axis)
 
 
 def from_behind(value, axis, by):

time: 1110 us -> 459 us (0.41)
  waiting for transfers between devices: 947 us -> 76.1 us
  blocking collectives: 0 us -> 251 us
  other arithmetic: 53.8 us -> 29 us
    psum x16 -> x0, waiting for transfers between devices: 870 us -> none  [broadcast(): return lax.psum(kept, axis)]
    all_gather x0 -> x16, blocking collectives: none -> 251 us  [_store_unit(): before = jnp.sum(lax.all_gather(local_values, net_axis), axis=0)]
    another operation x33 -> x17, other arithmetic: 35.5 us -> 10.4 us
  transfers between devices with their start and end apart: 22 -> 6, of which waited for: 21 -> 5; matrix products, arithmetic and copies ran while one was open for 1% -> 8% of each run, Pallas kernels for 0% -> 0%
where the time goes in v1:
time: 459 us; the launch traced here: 458 us
  blocking collectives  251 us (55%)
  waiting for transfers between devices  76.1 us (17%)
  loops' own time  40 us (9%)
  other arithmetic  29 us (6%)
  starting transfers between devices  20.2 us (4%)
  local copies, waits for them, and re-layouts  17.4 us (4%)
  between operations  13.7 us (3%)
  matrix products  11.4 us (2%)
    all_gather x16, blocking collectives, _store_unit(): before = jnp.sum(lax.all_gather(local_values, net_axis), axis=0)  251 us
    all_gather x1, waiting for transfers between devices, per_device(): gathered = lax.all_gather(hidden, 'kvh', axis=1, tiled=True)  38.8 us
    another operation x1, loops' own time, per_device(): lax.fori_loop(0, local_heads * vertical_count, fetch_block, start_buffer)  38.4 us
    ppermute x4, waiting for transfers between devices, from_behind(): return lax.ppermute(value, axis, pairs)  20.7 us
    ppermute x4, starting transfers between devices, from_behind(): return lax.ppermute(value, axis, pairs)  20.1 us
    all_gather x1, waiting for transfers between devices, per_device(): lax.all_gather(key_value_matrix, 'fsdp', axis=0, tiled=True)  15.2 us
    another operation x17, other arithmetic  10.4 us
    scatter x16, other arithmetic, fetch_block(): return buffer.at[head_index, slot_index].set(received)  9.73 us
  transfers between devices with their start and end apart: 6, of which 5 were waited for; matrix products, arithmetic and copies ran while one was open for 8% of the time, Pallas kernels for 0%

profile of v1, /device:TPU:0, one launch (start us, length us, event | category | flops | bytes accessed | tf_op | source)
XLA Modules:
  0.0 458.3 jit_solution(8719884779935344804)
XLA Ops:
  6.5 0.7 all-gather.6.cloned.1.call-update
  7.3 0.7 all-gather.8.cloned.1.call-update
  8.4 38.8 %all-gather.6.cloned.1.call-done = bf16[256,4096]{1,0:T(8,128)(2,1)} async-done(((bf16[256,1024]{1,0:T(8,128)(2,1)}), bf16[256,4096]{1,0:T(8,128)(2,1)}) %all-gather.6.cloned.1.call-update) | async-done | bytes 2097168 | tf_op jit(solution)/shard_map/all_gather | solution.py:48
  47.1 15.2 %all-gather.8.cloned.1.call-done = bf16[4096,512]{1,0:T(8,128)(2,1)} async-done(((bf16[2048,512]{1,0:T(8,128)(2,1)}), bf16[4096,512]{1,0:T(8,128)(2,1)}) %all-gather.8.cloned.1.call-update) | async-done | bytes 4194320 | tf_op jit(solution)/shard_map/all_gather | solution.py:51
  62.4 4.1 fusion.22
  68.7 2.2 collective-permute-start
  70.9 1.4 collective-permute-done
  72.4 0.7 broadcast_select_fusion
  73.0 10.5 %collective-permute-start.1 = (bf16[2,2,2,128,2,128]{5,2,4,3,1,0:T(2,128)(2,1)S(1)}, bf16[2,2,2,128,2,128]{5,2,4,3,1,0:T(2,128)(2,1)S(1)}, u32[]{:S(2)}, u32[]{:S(2)}) collective-permute-start(bf16[2,2,2,128,2,128]{5,2,4,3,1,0:T(2,128)(2,1)S(1)} %broadcast_select_fusion), channel_id=1, source_target_pairs={{0,8},{4,12},{8,16},{12,20},{16,24},{20,28},{1,9},{5,13},{9,17},{1... | collective-permute-start | bytes 1572872 | tf_op jit(solution)/shard_map/ppermute | solution.py:23
  84.0 10.0 %collective-permute-done.1 = bf16[2,2,2,128,2,128]{5,2,4,3,1,0:T(2,128)(2,1)S(1)} collective-permute-done((bf16[2,2,2,128,2,128]{5,2,4,3,1,0:T(2,128)(2,1)S(1)}, bf16[2,2,2,128,2,128]{5,2,4,3,1,0:T(2,128)(2,1)S(1)}, u32[]{:S(2)}, u32[]{:S(2)}) %collective-permute-start.1) | collective-permute-done | bytes 524320 | tf_op jit(solution)/shard_map/ppermute | solution.py:23
  94.0 0.8 broadcast_select_fusion.1
  94.8 5.3 %collective-permute-start.2 = (bf16[2,2,2,128,2,128]{5,2,4,3,1,0:T(2,128)(2,1)S(1)}, bf16[2,2,2,128,2,128]{5,2,4,3,1,0:T(2,128)(2,1)S(1)}, u32[]{:S(2)}, u32[]{:S(2)}) collective-permute-start(bf16[2,2,2,128,2,128]{5,2,4,3,1,0:T(2,128)(2,1)S(1)} %broadcast_select_fusion.1), channel_id=1, source_target_pairs={{0,16},{4,20},{8,24},{12,28},{1,17},{5,21},{9,25},{13,29},{2,18},{... | collective-permute-start | bytes 1572872 | tf_op jit(solution)/shard_map/ppermute | solution.py:23
  100.4 9.3 %collective-permute-done.2 = bf16[2,2,2,128,2,128]{5,2,4,3,1,0:T(2,128)(2,1)S(1)} collective-permute-done((bf16[2,2,2,128,2,128]{5,2,4,3,1,0:T(2,128)(2,1)S(1)}, bf16[2,2,2,128,2,128]{5,2,4,3,1,0:T(2,128)(2,1)S(1)}, u32[]{:S(2)}, u32[]{:S(2)}) %collective-permute-start.2) | collective-permute-done | bytes 524320 | tf_op jit(solution)/shard_map/ppermute | solution.py:23
  109.8 0.6 broadcast_select_fusion.2
  110.4 2.1 collective-permute-start.3
  112.7 321.6 %while.30 = (s32[]{:T(128)}, bf16[2,8,128,2,128]{4,2,1,0,3:T(8,128)(2,1)S(1)}, s32[2,8]{1,0:T(2,128)S(1)}, bf16[2,2,128,2,128]{4,2,3,1,0:T(8,128)(2,1)S(1)}, s32...) while((s32[]{:T(128)}, ...), condition=%wide.region_3.4_spmd, body=%wide.region_0.3_spmd.sunk | while | flops 294984 | bytes 1639211 | solution.py:78
  115.7 24.6 %all-gather.2 = bf16[8,1,128,2,128]{4,2,3,1,0:T(8,128)(2,1)S(1)} all-gather(bf16[1,1,128,2,128]{4,2,3,1,0:T(8,128)(2,1)S(1)} %dynamic-slice_select_fusion.2), channel_id=2, replica_groups=mesh['ctx'=4,'fsdp'=2,'kvh'=4] {'ctx','fsdp'}, dimensions={0}, use_global_device_ids=true | all-gather | bytes 589824 | tf_op jit(solution)/shard_map/while/body/eval_jaxpr/all_gather | solution.py:11
  140.5 0.6 and_reduce_fusion.2
  141.2 0.6 bitcast_dynamic-update-slice_fusion.2
  144.8 14.8 %all-gather.2 = bf16[8,1,128,2,128]{4,2,3,1,0:T(8,128)(2,1)S(1)} all-gather(bf16[1,1,128,2,128]{4,2,3,1,0:T(8,128)(2,1)S(1)} %dynamic-slice_select_fusion.2), channel_id=2, replica_groups=mesh['ctx'=4,'fsdp'=2,'kvh'=4] {'ctx','fsdp'}, dimensions={0}, use_global_device_ids=true | all-gather | bytes 589824 | tf_op jit(solution)/shard_map/while/body/eval_jaxpr/all_gather | solution.py:11
  159.8 0.6 and_reduce_fusion.2
  164.0 15.1 %all-gather.2 = bf16[8,1,128,2,128]{4,2,3,1,0:T(8,128)(2,1)S(1)} all-gather(bf16[1,1,128,2,128]{4,2,3,1,0:T(8,128)(2,1)S(1)} %dynamic-slice_select_fusion.2), channel_id=2, replica_groups=mesh['ctx'=4,'fsdp'=2,'kvh'=4] {'ctx','fsdp'}, dimensions={0}, use_global_device_ids=true | all-gather | bytes 589824 | tf_op jit(solution)/shard_map/while/body/eval_jaxpr/all_gather | solution.py:11
  179.3 0.6 and_reduce_fusion.2
  179.9 0.6 bitcast_dynamic-update-slice_fusion.2
  183.5 15.1 %all-gather.2 = bf16[8,1,128,2,128]{4,2,3,1,0:T(8,128)(2,1)S(1)} all-gather(bf16[1,1,128,2,128]{4,2,3,1,0:T(8,128)(2,1)S(1)} %dynamic-slice_select_fusion.2), channel_id=2, replica_groups=mesh['ctx'=4,'fsdp'=2,'kvh'=4] {'ctx','fsdp'}, dimensions={0}, use_global_device_ids=true | all-gather | bytes 589824 | tf_op jit(solution)/shard_map/while/body/eval_jaxpr/all_gather | solution.py:11
  198.8 0.6 and_reduce_fusion.2
  199.5 0.6 bitcast_dynamic-update-slice_fusion.2
  203.1 15.1 %all-gather.2 = bf16[8,1,128,2,128]{4,2,3,1,0:T(8,128)(2,1)S(1)} all-gather(bf16[1,1,128,2,128]{4,2,3,1,0:T(8,128)(2,1)S(1)} %dynamic-slice_select_fusion.2), channel_id=2, replica_groups=mesh['ctx'=4,'fsdp'=2,'kvh'=4] {'ctx','fsdp'}, dimensions={0}, use_global_device_ids=true | all-gather | bytes 589824 | tf_op jit(solution)/shard_map/while/body/eval_jaxpr/all_gather | solution.py:11
  218.3 0.6 and_reduce_fusion.2
  219.0 0.6 bitcast_dynamic-update-slice_fusion.2
  222.6 15.1 %all-gather.2 = bf16[8,1,128,2,128]{4,2,3,1,0:T(8,128)(2,1)S(1)} all-gather(bf16[1,1,128,2,128]{4,2,3,1,0:T(8,128)(2,1)S(1)} %dynamic-slice_select_fusion.2), channel_id=2, replica_groups=mesh['ctx'=4,'fsdp'=2,'kvh'=4] {'ctx','fsdp'}, dimensions={0}, use_global_device_ids=true | all-gather | bytes 589824 | tf_op jit(solution)/shard_map/while/body/eval_jaxpr/all_gather | solution.py:11
  237.8 0.6 and_reduce_fusion.2
  242.1 15.1 %all-gather.2 = bf16[8,1,128,2,128]{4,2,3,1,0:T(8,128)(2,1)S(1)} all-gather(bf16[1,1,128,2,128]{4,2,3,1,0:T(8,128)(2,1)S(1)} %dynamic-slice_select_fusion.2), channel_id=2, replica_groups=mesh['ctx'=4,'fsdp'=2,'kvh'=4] {'ctx','fsdp'}, dimensions={0}, use_global_device_ids=true | all-gather | bytes 589824 | tf_op jit(solution)/shard_map/while/body/eval_jaxpr/all_gather | solution.py:11
  257.4 0.6 and_reduce_fusion.2
  261.6 15.1 %all-gather.2 = bf16[8,1,128,2,128]{4,2,3,1,0:T(8,128)(2,1)S(1)} all-gather(bf16[1,1,128,2,128]{4,2,3,1,0:T(8,128)(2,1)S(1)} %dynamic-slice_select_fusion.2), channel_id=2, replica_groups=mesh['ctx'=4,'fsdp'=2,'kvh'=4] {'ctx','fsdp'}, dimensions={0}, use_global_device_ids=true | all-gather | bytes 589824 | tf_op jit(solution)/shard_map/while/body/eval_jaxpr/all_gather | solution.py:11
  276.9 0.6 and_reduce_fusion.2
  281.2 15.1 %all-gather.2 = bf16[8,1,128,2,128]{4,2,3,1,0:T(8,128)(2,1)S(1)} all-gather(bf16[1,1,128,2,128]{4,2,3,1,0:T(8,128)(2,1)S(1)} %dynamic-slice_select_fusion.2), channel_id=2, replica_groups=mesh['ctx'=4,'fsdp'=2,'kvh'=4] {'ctx','fsdp'}, dimensions={0}, use_global_device_ids=true | all-gather | bytes 589824 | tf_op jit(solution)/shard_map/while/body/eval_jaxpr/all_gather | solution.py:11
  296.4 0.6 and_reduce_fusion.2
  300.7 15.1 %all-gather.2 = bf16[8,1,128,2,128]{4,2,3,1,0:T(8,128)(2,1)S(1)} all-gather(bf16[1,1,128,2,128]{4,2,3,1,0:T(8,128)(2,1)S(1)} %dynamic-slice_select_fusion.2), channel_id=2, replica_groups=mesh['ctx'=4,'fsdp'=2,'kvh'=4] {'ctx','fsdp'}, dimensions={0}, use_global_device_ids=true | all-gather | bytes 589824 | tf_op jit(solution)/shard_map/while/body/eval_jaxpr/all_gather | solution.py:11
  315.9 0.6 and_reduce_fusion.2
  320.2 15.1 %all-gather.2 = bf16[8,1,128,2,128]{4,2,3,1,0:T(8,128)(2,1)S(1)} all-gather(bf16[1,1,128,2,128]{4,2,3,1,0:T(8,128)(2,1)S(1)} %dynamic-slice_select_fusion.2), channel_id=2, replica_groups=mesh['ctx'=4,'fsdp'=2,'kvh'=4] {'ctx','fsdp'}, dimensions={0}, use_global_device_ids=true | all-gather | bytes 589824 | tf_op jit(solution)/shard_map/while/body/eval_jaxpr/all_gather | solution.py:11
  335.5 0.6 and_reduce_fusion.2
  339.7 15.1 %all-gather.2 = bf16[8,1,128,2,128]{4,2,3,1,0:T(8,128)(2,1)S(1)} all-gather(bf16[1,1,128,2,128]{4,2,3,1,0:T(8,128)(2,1)S(1)} %dynamic-slice_select_fusion.2), channel_id=2, replica_groups=mesh['ctx'=4,'fsdp'=2,'kvh'=4] {'ctx','fsdp'}, dimensions={0}, use_global_device_ids=true | all-gather | bytes 589824 | tf_op jit(solution)/shard_map/while/body/eval_jaxpr/all_gather | solution.py:11
  355.0 0.6 and_reduce_fusion.2
  359.2 15.1 %all-gather.2 = bf16[8,1,128,2,128]{4,2,3,1,0:T(8,128)(2,1)S(1)} all-gather(bf16[1,1,128,2,128]{4,2,3,1,0:T(8,128)(2,1)S(1)} %dynamic-slice_select_fusion.2), channel_id=2, replica_groups=mesh['ctx'=4,'fsdp'=2,'kvh'=4] {'ctx','fsdp'}, dimensions={0}, use_global_device_ids=true | all-gather | bytes 589824 | tf_op jit(solution)/shard_map/while/body/eval_jaxpr/all_gather | solution.py:11
  374.5 0.6 and_reduce_fusion.2
  378.8 15.1 %all-gather.2 = bf16[8,1,128,2,128]{4,2,3,1,0:T(8,128)(2,1)S(1)} all-gather(bf16[1,1,128,2,128]{4,2,3,1,0:T(8,128)(2,1)S(1)} %dynamic-slice_select_fusion.2), channel_id=2, replica_groups=mesh['ctx'=4,'fsdp'=2,'kvh'=4] {'ctx','fsdp'}, dimensions={0}, use_global_device_ids=true | all-gather | bytes 589824 | tf_op jit(solution)/shard_map/while/body/eval_jaxpr/all_gather | solution.py:11
  394.0 0.6 and_reduce_fusion.2
  398.3 15.1 %all-gather.2 = bf16[8,1,128,2,128]{4,2,3,1,0:T(8,128)(2,1)S(1)} all-gather(bf16[1,1,128,2,128]{4,2,3,1,0:T(8,128)(2,1)S(1)} %dynamic-slice_select_fusion.2), channel_id=2, replica_groups=mesh['ctx'=4,'fsdp'=2,'kvh'=4] {'ctx','fsdp'}, dimensions={0}, use_global_device_ids=true | all-gather | bytes 589824 | tf_op jit(solution)/shard_map/while/body/eval_jaxpr/all_gather | solution.py:11
  413.6 0.6 and_reduce_fusion.2
  417.8 15.1 %all-gather.2 = bf16[8,1,128,2,128]{4,2,3,1,0:T(8,128)(2,1)S(1)} all-gather(bf16[1,1,128,2,128]{4,2,3,1,0:T(8,128)(2,1)S(1)} %dynamic-slice_select_fusion.2), channel_id=2, replica_groups=mesh['ctx'=4,'fsdp'=2,'kvh'=4] {'ctx','fsdp'}, dimensions={0}, use_global_device_ids=true | all-gather | bytes 589824 | tf_op jit(solution)/shard_map/while/body/eval_jaxpr/all_gather | solution.py:11
  433.1 0.6 and_reduce_fusion.2
  435.0 2.3 fusion.10
  437.3 14.1 %while.31 = (s32[]{:T(128)}, bf16[2,128,1024]{2,1,0:T(8,128)(2,1)}, bf16[2,2,128,2,128]{4,2,1,3,0:T(8,128)(2,1)S(1)}, bf16[2,2,2,128,2,128]{5,3,2,1,4,0:T(8,128)...) while((s32[]{:T(128)}, bf16[2,128,1024]{2,1,0:T(8,128)(2,1)}, ...), condition=%wide.region_8.9_spmd.clone, body=%wide.region_4.8_spmd.clone.sunk | while | flops 757610624 | bytes 26350708 | solution.py:142
  437.4 0.7 dynamic_slice.64
  439.7 0.9 fusion.30
  440.6 1.3 fusion.31
  441.9 1.6 fusion.32
  443.7 0.7 constant_dynamic-update-slice_fusion.2
  444.4 0.7 dynamic_slice.64
  446.7 0.9 fusion.30
  447.7 1.3 fusion.31
  449.0 1.6 fusion.32
  450.7 0.7 constant_dynamic-update-slice_fusion.2
  (159 shorter events, 26.1 us)
Async XLA Ops:
  6.5 40.6 %all-gather.6.cloned.1.call-start = ((), (), s32[]{:S(2)}) async-start(), calls=%async_computation | async-start | bytes 2621440 | tf_op jit(solution)/shard_map/all_gather | solution.py:48
  7.3 55.1 %all-gather.8.cloned.1.call-start = ((), (), s32[]{:S(2)}) async-start(), calls=%async_computation.1 | async-start | bytes 6291456 | tf_op jit(solution)/shard_map/all_gather | solution.py:51
  66.4 4.5 copy-start.2
  66.4 17.2 %copy-start = (bf16[256,1024]{1,0:T(8,128)(2,1)S(1)}, bf16[256,1024]{1,0:T(8,128)(2,1)}, u32[]{:S(2)}) copy-start(bf16[256,1024]{1,0:T(8,128)(2,1)} %param.13) | copy-start | bytes 1572868
  68.4 44.3 %copy-start.1 = (s32[2,8]{1,0:T(2,128)S(1)}, s32[2,8]{1,0:T(2,128)}, u32[]{:S(2)}) copy-start(s32[2,8]{1,0:T(2,128)} %param.14) | copy-start | bytes 196
  68.4 44.3 %copy-start.3 = (s32[5]{0:T(128)S(1)}, s32[5]{0:T(128)}, u32[]{:S(2)}) copy-start(s32[5]{0:T(128)} %constant.409.clone.1) | copy-start | bytes 64
  68.7 3.7 collective-permute-start
  73.0 21.0 %collective-permute-start.1 = (bf16[2,2,2,128,2,128]{5,2,4,3,1,0:T(2,128)(2,1)S(1)}, bf16[2,2,2,128,2,128]{5,2,4,3,1,0:T(2,128)(2,1)S(1)}, u32[]{:S(2)}, u32[]{:S(2)}) collective-permute-start(bf16[2,2,2,128,2,128]{5,2,4,3,1,0:T(2,128)(2,1)S(1)} %broadcast_select_fusion), channel_id=1, source_target_pairs={{0,8},{4,12},{8,16},{12,20},{16,24},{20,28},{1,9},{5,13},{9,17},{1... | collective-permute-start | bytes 1572872 | tf_op jit(solution)/shard_map/ppermute | solution.py:23
  94.8 15.0 %collective-permute-start.2 = (bf16[2,2,2,128,2,128]{5,2,4,3,1,0:T(2,128)(2,1)S(1)}, bf16[2,2,2,128,2,128]{5,2,4,3,1,0:T(2,128)(2,1)S(1)}, u32[]{:S(2)}, u32[]{:S(2)}) collective-permute-start(bf16[2,2,2,128,2,128]{5,2,4,3,1,0:T(2,128)(2,1)S(1)} %broadcast_select_fusion.1), channel_id=1, source_target_pairs={{0,16},{4,20},{8,24},{12,28},{1,17},{5,21},{9,25},{13,29},{2,18},{... | collective-permute-start | bytes 1572872 | tf_op jit(solution)/shard_map/ppermute | solution.py:23
  110.4 324.6 %collective-permute-start.3 = (bf16[2,2,2,128,2,128]{5,2,4,3,1,0:T(2,128)(2,1)S(1)}, bf16[2,2,2,128,2,128]{5,2,4,3,1,0:T(2,128)(2,1)}, u32[]{:S(2)}, u32[]{:S(2)}) collective-permute-start(bf16[2,2,2,128,2,128]{5,2,4,3,1,0:T(2,128)(2,1)S(1)} %broadcast_select_fusion.2), channel_id=1, source_target_pairs={{0,4},{4,8},{8,12},{12,16},{16,20},{20,24},{24,28},{1,5},{5,9},{9,... | collective-permute-start | bytes 1572872 | tf_op jit(solution)/shard_map/ppermute | solution.py:23
Sparse Core Ops, SparseCore 0:
  9.2 37.8 all-gather.5
  48.7 13.6 all-gather.7
